TPU v7x, 256 devices: a whole 4x4x8 slice. The times are simulated.
256 devices in a mesh: row: 16 (over y, x), col: 16 (over z, core).
Axes of the slice: x: 4, y: 4, z: 8, core: 2. Of those that a mesh axis runs over, the one named last changes fastest.
Arguments:
- block_values: float32 [16, 16, 40, 128, 128], P('row', 'col'), may hold values from 7.8125e-06 to 0.00078125
- block_index: int32 [16, 16, 2, 40], P('row', 'col'), may hold values from 0 to 31, as said below
- block_count: int32 [16, 16], P('row', 'col'), may hold values from 1 to 40, as said below
- strength: float32 [32], replicated, may hold values from 1 to 30
- raw_scores: float32 [512, 32, 128], P(('row', 'col')), may hold values from -24 to 24
Outputs:
- smoothed: float32 [512, 32, 128], P(('row', 'col'))
- final_residual: float32 [512, 32, 128], P(('row', 'col'))
Inputs may be any that keep to these rules, and one draw needn't show every extreme that they name: `block_count`: some device has exactly 40 live slots; the others hold between half and all of their share of the upper triangle, scaled to 40. `block_index`: the live slots of one device name distinct blocks, each with global block row at most its global block column; slots at or above the count hold pairs in range that are ignored.
All inputs are finite; a program needn't handle non-finite values.
Results may differ from a plain program's by a relative error of at most 0.0003.
Values sent between devices are 32-bit elements; how exact they have to be, the bound alone decides.
A program may use at most 64 MiB of HBM per device.

v0:
```python
import jax
import jax.numpy as jnp
from jax import lax
from jax.sharding import PartitionSpec as P

ITERS = 3


def local_terms(values, row_index, col_index, panel_rows, panel_cols):
    picked_cols = jnp.take(panel_cols, col_index, axis=0)
    picked_rows = jnp.take(panel_rows, row_index, axis=0)
    to_rows = jnp.einsum("crk,cik->cri", picked_cols, values, precision=lax.Precision.HIGHEST)
    to_cols = jnp.einsum("cri,cik->crk", picked_rows, values, precision=lax.Precision.HIGHEST)
    row_part = jax.ops.segment_sum(to_rows, row_index, num_segments=panel_rows.shape[0])
    col_part = jax.ops.segment_sum(to_cols, col_index, num_segments=panel_cols.shape[0])
    return (row_part, col_part)


def fold_terms(row_part, col_part):
    return lax.psum_scatter(row_part, "col", scatter_dimension=0, tiled=True) + lax.psum_scatter(
        col_part, "row", scatter_dimension=0, tiled=True
    )


def total(field):
    return jnp.sum(field, axis=(0, 2))


def global_sum(partial_sum):
    return lax.psum(partial_sum, ("row", "col"))


def shards(block_values, block_index, block_count, strength, raw_scores):
    values = block_values[0, 0]
    row_index = block_index[0, 0, 0]
    col_index = block_index[0, 0, 1]
    live_mask = (jnp.arange(values.shape[0], dtype=jnp.int32) < block_count[0, 0]).astype(
        jnp.float32
    )
    masked = values * live_mask[:, None, None]
    segment = raw_scores.shape[0]
    block_size = raw_scores.shape[2]
    rows_here = lax.axis_size("col") * segment
    cols_here = lax.axis_size("row") * segment
    ones_rows = jnp.ones((rows_here, 1, block_size), jnp.float32)
    ones_cols = jnp.ones((cols_here, 1, block_size), jnp.float32)
    degree_rows, degree_cols = local_terms(masked, row_index, col_index, ones_rows, ones_cols)
    degree = fold_terms(degree_rows, degree_cols)
    gains = strength[None, :, None]
    smoothed = jnp.zeros_like(raw_scores)
    residual = raw_scores
    direction = raw_scores
    norm_now = global_sum(total(residual * residual))
    for iteration in range(ITERS):
        panel_rows = lax.all_gather(direction, "col", axis=0, tiled=True)
        panel_cols = lax.all_gather(direction, "row", axis=0, tiled=True)
        row_part, col_part = local_terms(masked, row_index, col_index, panel_rows, panel_cols)
        product = fold_terms(row_part, col_part)
        image = direction + gains * (degree * direction - product)
        step_size = norm_now / global_sum(total(direction * image))
        smoothed = smoothed + step_size[None, :, None] * direction
        residual = residual - step_size[None, :, None] * image
        norm_next = global_sum(total(residual * residual))
        direction = residual + (norm_next / norm_now)[None, :, None] * direction
        norm_now = norm_next
    return (smoothed, residual)


def solution(mesh):
    placed = (
        P("row", "col", None, None, None),
        P("row", "col", None, None),
        P("row", "col"),
        P(),
        P(("row", "col"), None, None),
    )
    return jax.shard_map(
        shards,
        mesh=mesh,
        in_specs=placed,
        out_specs=(P(("row", "col"), None, None), P(("row", "col"), None, None)),
        check_vma=False,
    )
```

profile of v0, /device:TPU:1, one launch (start us, length us, event | category | flops | bytes accessed | tf_op | source)
XLA Modules:
  0.0 916.9 jit_solution(5695150841030016190)
XLA Ops:
  9.4 23.0 %all_gather.19 = f32[32,32,128]{2,1,0:T(8,128)S(1)} all-gather(f32[2,32,128]{2,1,0:T(8,128)} %param.13), channel_id=1, replica_groups=mesh['row'=16,'col'=16] {'col'}, dimensions={0}, use_global_device_ids=true | all-gather | bytes 557056 | tf_op jit(solution)/shard_map/all_gather | solution.py:55
  33.0 5.0 fusion.4
  38.1 4.9 scatter_fusion.1
  43.9 19.6 %all_gather.18 = f32[32,32,128]{2,1,0:T(8,128)S(1)} all-gather(f32[2,32,128]{2,1,0:T(8,128)S(1)} %copy-done.7), channel_id=1, replica_groups=mesh['row'=16,'col'=16] {'row'}, dimensions={0}, use_global_device_ids=true | all-gather | bytes 557056 | tf_op jit(solution)/shard_map/all_gather | solution.py:56
  64.9 6.2 fusion.5
  71.1 4.7 scatter_fusion
  80.5 4.3 fusion.7
  85.7 2.3 fusion.6
  88.7 58.4 %all-reduce.1 = f32[32,1,128]{2,0,1:T(8,128)S(1)} all-reduce(f32[32,1,128]{2,0,1:T(8,128)S(1)} %bitcast.49), channel_id=3, replica_groups=mesh['row'=16,'col'=16] {'row'}, use_global_device_ids=true, to_apply=%region_5.7.clone | all-reduce | flops 4096 | bytes 32768
  147.1 61.3 %all-reduce = f32[32,1,128]{2,0,1:T(8,128)S(1)} all-reduce(f32[32,1,128]{2,0,1:T(8,128)S(1)} %bitcast.48), channel_id=2, replica_groups=mesh['row'=16,'col'=16] {'col'}, use_global_device_ids=true, to_apply=%region_3.5.clone | all-reduce | flops 4096 | bytes 32768
  209.5 74.0 %all-reduce.2 = (f32[32]{0:T(128)S(1)}, f32[32]{0:T(128)S(1)}) all-reduce(f32[32]{0:T(128)S(1)} %get-tuple-element.5, f32[32]{0:T(128)S(1)} %get-tuple-element.4), channel_id=1, replica_groups=mesh['row'=16,'col'=16] {'row','col'}, use_global_device_ids=true, to_apply=%region_1.2 | all-reduce | flops 64 | bytes 512 | tf_op jit(solution)/shard_map/psum | solution.py:30
  284.5 74.5 %psum.44 = f32[32]{0:T(128)S(1)} all-reduce(f32[32]{0:T(128)S(1)} %get-tuple-element.10), channel_id=1, replica_groups=mesh['row'=16,'col'=16] {'row','col'}, use_global_device_ids=true, to_apply=%region_13.16 | all-reduce | flops 32 | bytes 256 | tf_op jit(solution)/shard_map/psum | solution.py:30
  359.0 17.2 %all_gather.21 = f32[32,32,128]{2,1,0:T(8,128)S(1)} all-gather(f32[2,32,128]{2,1,0:T(8,128)S(1)} %multiply_add_fusion.4), channel_id=1, replica_groups=mesh['row'=16,'col'=16] {'col'}, dimensions={0}, use_global_device_ids=true | all-gather | bytes 557056 | tf_op jit(solution)/shard_map/all_gather | solution.py:55
  377.7 4.3 fusion.2
  382.1 4.7 scatter_fusion.3
  387.7 19.2 %all_gather.20 = f32[32,32,128]{2,1,0:T(8,128)S(1)} all-gather(f32[2,32,128]{2,1,0:T(8,128)S(1)} %multiply_add_fusion.4), channel_id=1, replica_groups=mesh['row'=16,'col'=16] {'row'}, dimensions={0}, use_global_device_ids=true | all-gather | bytes 557056 | tf_op jit(solution)/shard_map/all_gather | solution.py:56
  408.3 6.2 fusion.3
  414.5 4.7 scatter_fusion.2
  420.1 38.4 %reduce-scatter.15.cloned.1.call-done = f32[2,32,128]{2,1,0:T(8,128)} async-done(((f32[32,32,128]{2,1,0:T(8,128)}), f32[2,32,128]{2,1,0:T(8,128)}) %reduce-scatter.15.cloned.1.call-update) | async-done | bytes 32784 | tf_op jit(solution)/shard_map/reduce_scatter | solution.py:20
  458.5 57.2 %reduce-scatter.13.cloned.1.call-done = f32[2,32,128]{2,1,0:T(8,128)} async-done(((f32[32,32,128]{2,1,0:T(8,128)}), f32[2,32,128]{2,1,0:T(8,128)}) %reduce-scatter.13.cloned.1.call-update) | async-done | bytes 32784 | tf_op jit(solution)/shard_map/reduce_scatter | solution.py:20
  516.7 79.6 %psum.45 = f32[32]{0:T(128)S(1)} all-reduce(f32[32]{0:T(128)S(1)} %multiply_reduce_fusion.2), channel_id=1, replica_groups=mesh['row'=16,'col'=16] {'row','col'}, use_global_device_ids=true, to_apply=%region_19.22 | all-reduce | flops 32 | bytes 256 | tf_op jit(solution)/shard_map/psum | solution.py:30
  597.2 72.4 %psum.46 = f32[32]{0:T(128)S(1)} all-reduce(f32[32]{0:T(128)S(1)} %get-tuple-element.8), channel_id=1, replica_groups=mesh['row'=16,'col'=16] {'row','col'}, use_global_device_ids=true, to_apply=%region_21.24 | all-reduce | flops 32 | bytes 256 | tf_op jit(solution)/shard_map/psum | solution.py:30
  669.6 18.1 %all_gather.23 = f32[32,32,128]{2,1,0:T(8,128)S(1)} all-gather(f32[2,32,128]{2,1,0:T(8,128)S(1)} %multiply_add_fusion.2), channel_id=1, replica_groups=mesh['row'=16,'col'=16] {'col'}, dimensions={0}, use_global_device_ids=true | all-gather | bytes 557056 | tf_op jit(solution)/shard_map/all_gather | solution.py:55
  689.2 4.3 fusion
  693.6 4.7 scatter_fusion.5
  699.1 19.2 %all_gather.22 = f32[32,32,128]{2,1,0:T(8,128)S(1)} all-gather(f32[2,32,128]{2,1,0:T(8,128)S(1)} %multiply_add_fusion.2), channel_id=1, replica_groups=mesh['row'=16,'col'=16] {'row'}, dimensions={0}, use_global_device_ids=true | all-gather | bytes 557056 | tf_op jit(solution)/shard_map/all_gather | solution.py:56
  719.8 5.3 fusion.1
  725.2 2.7 scatter_fusion.4
  728.7 41.8 %reduce-scatter.19.cloned.1.call-done = f32[2,32,128]{2,1,0:T(8,128)} async-done(((f32[32,32,128]{2,1,0:T(8,128)}), f32[2,32,128]{2,1,0:T(8,128)}) %reduce-scatter.19.cloned.1.call-update) | async-done | bytes 32784 | tf_op jit(solution)/shard_map/reduce_scatter | solution.py:20
  770.5 57.3 %reduce-scatter.17.cloned.1.call-done = f32[2,32,128]{2,1,0:T(8,128)} async-done(((f32[32,32,128]{2,1,0:T(8,128)}), f32[2,32,128]{2,1,0:T(8,128)}) %reduce-scatter.17.cloned.1.call-update) | async-done | bytes 32784 | tf_op jit(solution)/shard_map/reduce_scatter | solution.py:20
  828.8 79.8 %psum.47 = f32[32]{0:T(128)S(1)} all-reduce(f32[32]{0:T(128)S(1)} %multiply_reduce_fusion), channel_id=1, replica_groups=mesh['row'=16,'col'=16] {'row','col'}, use_global_device_ids=true, to_apply=%region_27.30 | all-reduce | flops 32 | bytes 256 | tf_op jit(solution)/shard_map/psum | solution.py:30
  908.5 1.5 multiply_subtract_fusion
  (74 shorter events, 23.8 us)
Async XLA Ops:
  7.2 201.3 %reduce-scatter.11.cloned.1.call-start = ((), (), s32[]{:S(2)}) async-start(), calls=%async_computation.7 | async-start | bytes 557056 | tf_op jit(solution)/shard_map/reduce_scatter | solution.py:20
  33.0 10.9 %copy-start.7 = (f32[2,32,128]{2,1,0:T(8,128)S(1)}, f32[2,32,128]{2,1,0:T(8,128)}, u32[]{:S(2)}) copy-start(f32[2,32,128]{2,1,0:T(8,128)} %param.13) | copy-start | bytes 98308
  38.0 26.9 %copy-start = (f32[1,1,40,128,128]{4,3,2,1,0:T(8,128)S(1)}, f32[1,1,40,128,128]{4,3,2,1,0:T(8,128)}, u32[]{:S(2)}) copy-start(f32[1,1,40,128,128]{4,3,2,1,0:T(8,128)} %param.9) | copy-start | bytes 7864324
  42.9 0.8 copy-start.3
  43.8 164.7 %reduce-scatter.9.cloned.1.call-start = ((), (), s32[]{:S(2)}) async-start(), calls=%async_computation.6 | async-start | bytes 557056 | tf_op jit(solution)/shard_map/reduce_scatter | solution.py:20
  71.1 6.8 copy-start.10
  71.1 7.4 copy-start.9
  75.8 0.8 copy-start.4
  76.7 381.8 %reduce-scatter.15.cloned.1.call-start = ((), (), s32[]{:S(2)}) async-start(), calls=%async_computation.9 | async-start | bytes 557056 | tf_op jit(solution)/shard_map/reduce_scatter | solution.py:20
  80.4 128.1 %copy-start.8 = (f32[32]{0:T(128)S(1)}, f32[32]{0:T(128)}, u32[]{:S(2)}) copy-start(f32[32]{0:T(128)} %param.12) | copy-start | bytes 388
  386.8 0.8 copy-start.5
  387.6 128.1 %reduce-scatter.13.cloned.1.call-start = ((), (), s32[]{:S(2)}) async-start(), calls=%async_computation.8 | async-start | bytes 557056 | tf_op jit(solution)/shard_map/reduce_scatter | solution.py:20
  419.2 0.8 copy-start.6
  420.0 350.5 %reduce-scatter.19.cloned.1.call-start = ((), (), s32[]{:S(2)}) async-start(), calls=%async_computation.11 | async-start | bytes 557056 | tf_op jit(solution)/shard_map/reduce_scatter | solution.py:20
  698.3 0.8 copy-start.2
  699.1 128.7 %reduce-scatter.17.cloned.1.call-start = ((), (), s32[]{:S(2)}) async-start(), calls=%async_computation.10 | async-start | bytes 557056 | tf_op jit(solution)/shard_map/reduce_scatter | solution.py:20
  727.9 0.8 copy-start.1
Sparse Core Ops, SparseCore 0:
  43.9 73.4 reduce-scatter.10
  120.0 55.2 reduce-scatter.8
  387.7 70.6 reduce-scatter.14
  461.0 54.6 reduce-scatter.12
  699.2 71.2 reduce-scatter.18
  773.0 54.7 reduce-scatter.16
where the time goes:
time: 918 us; the launch traced here: 917 us
  blocking collectives  616 us (67%)
  waiting for transfers between devices  195 us (21%)
  matrix products  37.9 us (4%)
  other arithmetic  35.4 us (4%)
  between operations  16.3 us (2%)
  local copies, waits for them, and re-layouts  15.9 us (2%)
    psum x5, blocking collectives, global_sum(): return lax.psum(partial_sum, ('row', 'col'))  380 us
    unnamed x2, blocking collectives  120 us
    reduce_scatter x3, waiting for transfers between devices, fold_terms(): lax.psum_scatter(row_part, 'col', scatter_dimension=0, tiled=True)  115 us
    reduce_scatter x3, waiting for transfers between devices, fold_terms(): lax.psum_scatter(col_part, 'row', scatter_dimension=0, tiled=True)  80.2 us
    all_gather x3, blocking collectives, shards(): panel_rows = lax.all_gather(direction, 'col', axis=0, tiled=True)  58.3 us
    all_gather x3, blocking collectives, shards(): panel_cols = lax.all_gather(direction, 'row', axis=0, tiled=True)  58 us
    dot_general x4, matrix products, local_terms(): jnp.einsum('crk,cik->cri', picked_cols, values, precision=lax.Precision.H...  22 us
  transfers between devices with their start and end apart: 6, of which 4 were waited for; matrix products, arithmetic and copies ran while one was open for 5% of the time, Pallas kernels for 0%

commit v1 on v0

--- a/solution.py
+++ b/solution.py
@@ -27,7 +27,12 @@
 
 
 def global_sum(partial_sum):
-    return lax.psum(partial_sum, ("row", "col"))
+
+    def drive_sample_up(mat, dev_axis, lane_axis):
+        aux = lax.psum(lax.psum(mat, axis_name=dev_axis), axis_name=lane_axis)
+        return aux
+
+    return drive_sample_up(partial_sum, "col", "row")
 
 
 def shards(block_values, block_index, block_count, strength, raw_scores):

time: 918 us -> 848 us (0.924)
  blocking collectives: 616 us -> 540 us
    psum x5 -> x10, blocking collectives: 380 us -> 294 us  [drive_sample_up(): aux = lax.psum(lax.psum(mat, axis_name=dev_axis), axis_name=lane_axis)]
    all_gather x3, blocking collectives: 58.3 us -> 70.5 us  [shards(): panel_rows = lax.all_gather(direction, 'col', axis=0, tiled=True)]
where the time goes in v1:
time: 848 us; the launch traced here: 842 us
  blocking collectives  540 us (64%)
  waiting for transfers between devices  197 us (23%)
  matrix products  37.9 us (4%)
  other arithmetic  35.4 us (4%)
  between operations  16.3 us (2%)
  local copies, waits for them, and re-layouts  15.9 us (2%)
    psum x10, blocking collectives, drive_sample_up(): aux = lax.psum(lax.psum(mat, axis_name=dev_axis), axis_name=lane_axis)  294 us
    unnamed x2, blocking collectives  120 us
    reduce_scatter x3, waiting for transfers between devices, fold_terms(): lax.psum_scatter(row_part, 'col', scatter_dimension=0, tiled=True)  114 us
    reduce_scatter x3, waiting for transfers between devices, fold_terms(): lax.psum_scatter(col_part, 'row', scatter_dimension=0, tiled=True)  82.1 us
    all_gather x3, blocking collectives, shards(): panel_rows = lax.all_gather(direction, 'col', axis=0, tiled=True)  70.5 us
    all_gather x3, blocking collectives, shards(): panel_cols = lax.all_gather(direction, 'row', axis=0, tiled=True)  55.3 us
    dot_general x4, matrix products, local_terms(): jnp.einsum('crk,cik->cri', picked_cols, values, precision=lax.Precision.H...  22 us
  transfers between devices with their start and end apart: 6, of which 4 were waited for; matrix products, arithmetic and copies ran while one was open for 5% of the time, Pallas kernels for 0%

profile of v1, /device:TPU:1, one launch (start us, length us, event | category | flops | bytes accessed | tf_op | source)
XLA Modules:
  0.0 842.0 jit_solution(9813179164585319551)
XLA Ops:
  9.4 23.0 %all_gather.19 = f32[32,32,128]{2,1,0:T(8,128)S(1)} all-gather(f32[2,32,128]{2,1,0:T(8,128)} %param.13), channel_id=1, replica_groups=mesh['row'=16,'col'=16] {'col'}, dimensions={0}, use_global_device_ids=true | all-gather | bytes 557056 | tf_op jit(solution)/shard_map/all_gather | solution.py:60
  33.0 5.0 fusion.4
  38.1 4.9 scatter_fusion.1
  43.9 19.6 %all_gather.18 = f32[32,32,128]{2,1,0:T(8,128)S(1)} all-gather(f32[2,32,128]{2,1,0:T(8,128)S(1)} %copy-done.7), channel_id=1, replica_groups=mesh['row'=16,'col'=16] {'row'}, dimensions={0}, use_global_device_ids=true | all-gather | bytes 557056 | tf_op jit(solution)/shard_map/all_gather | solution.py:61
  64.9 6.2 fusion.5
  71.1 4.7 scatter_fusion
  88.7 58.4 %all-reduce.1 = f32[32,1,128]{2,0,1:T(8,128)S(1)} all-reduce(f32[32,1,128]{2,0,1:T(8,128)S(1)} %bitcast.49), channel_id=3, replica_groups=mesh['row'=16,'col'=16] {'row'}, use_global_device_ids=true, to_apply=%region_6.8.clone | all-reduce | flops 4096 | bytes 32768
  147.1 61.3 %all-reduce = f32[32,1,128]{2,0,1:T(8,128)S(1)} all-reduce(f32[32,1,128]{2,0,1:T(8,128)S(1)} %bitcast.48), channel_id=2, replica_groups=mesh['row'=16,'col'=16] {'col'}, use_global_device_ids=true, to_apply=%region_4.6.clone | all-reduce | flops 4096 | bytes 32768
  209.5 26.4 %all-reduce.2 = (f32[32]{0:T(128)S(1)}, f32[32]{0:T(128)S(1)}) all-reduce(f32[32]{0:T(128)S(1)} %get-tuple-element.5, f32[32]{0:T(128)S(1)} %get-tuple-element.4), channel_id=1, replica_groups=mesh['row'=16,'col'=16] {'col'}, use_global_device_ids=true, to_apply=%region_1.2 | all-reduce | flops 64 | bytes 512 | tf_op jit(solution)/shard_map/psum | solution.py:32
  235.9 28.5 %all-reduce.3 = (f32[32]{0:T(128)S(1)}, f32[32]{0:T(128)S(1)}) all-reduce(f32[32]{0:T(128)S(1)} %get-tuple-element.6, f32[32]{0:T(128)S(1)} %get-tuple-element.7), channel_id=1, replica_groups=mesh['row'=16,'col'=16] {'row'}, use_global_device_ids=true, to_apply=%region_2.3 | all-reduce | flops 64 | bytes 512 | tf_op jit(solution)/shard_map/psum | solution.py:32
  265.4 30.5 %psum.88 = f32[32]{0:T(128)S(1)} all-reduce(f32[32]{0:T(128)S(1)} %get-tuple-element.12), channel_id=1, replica_groups=mesh['row'=16,'col'=16] {'col'}, use_global_device_ids=true, to_apply=%region_15.18 | all-reduce | flops 32 | bytes 256 | tf_op jit(solution)/shard_map/psum | solution.py:32
  295.9 30.2 %psum.89 = f32[32]{0:T(128)S(1)} all-reduce(f32[32]{0:T(128)S(1)} %psum.88), channel_id=1, replica_groups=mesh['row'=16,'col'=16] {'row'}, use_global_device_ids=true, to_apply=%region_16.19 | all-reduce | flops 32 | bytes 256 | tf_op jit(solution)/shard_map/psum | solution.py:32
  326.2 23.4 %all_gather.21 = f32[32,32,128]{2,1,0:T(8,128)S(1)} all-gather(f32[2,32,128]{2,1,0:T(8,128)S(1)} %multiply_add_fusion.4), channel_id=1, replica_groups=mesh['row'=16,'col'=16] {'col'}, dimensions={0}, use_global_device_ids=true | all-gather | bytes 557056 | tf_op jit(solution)/shard_map/all_gather | solution.py:60
  351.0 4.3 fusion.2
  355.4 4.7 scatter_fusion.3
  361.0 16.7 %all_gather.20 = f32[32,32,128]{2,1,0:T(8,128)S(1)} all-gather(f32[2,32,128]{2,1,0:T(8,128)S(1)} %multiply_add_fusion.4), channel_id=1, replica_groups=mesh['row'=16,'col'=16] {'row'}, dimensions={0}, use_global_device_ids=true | all-gather | bytes 557056 | tf_op jit(solution)/shard_map/all_gather | solution.py:61
  379.2 6.2 fusion.3
  385.4 4.7 scatter_fusion.2
  391.0 38.7 %reduce-scatter.15.cloned.1.call-done = f32[2,32,128]{2,1,0:T(8,128)} async-done(((f32[32,32,128]{2,1,0:T(8,128)}), f32[2,32,128]{2,1,0:T(8,128)}) %reduce-scatter.15.cloned.1.call-update) | async-done | bytes 32784 | tf_op jit(solution)/shard_map/reduce_scatter | solution.py:20
  429.7 57.2 %reduce-scatter.13.cloned.1.call-done = f32[2,32,128]{2,1,0:T(8,128)} async-done(((f32[32,32,128]{2,1,0:T(8,128)}), f32[2,32,128]{2,1,0:T(8,128)}) %reduce-scatter.13.cloned.1.call-update) | async-done | bytes 32784 | tf_op jit(solution)/shard_map/reduce_scatter | solution.py:20
  487.9 26.4 %psum.90 = f32[32]{0:T(128)S(1)} all-reduce(f32[32]{0:T(128)S(1)} %multiply_reduce_fusion.2), channel_id=1, replica_groups=mesh['row'=16,'col'=16] {'col'}, use_global_device_ids=true, to_apply=%region_22.25 | all-reduce | flops 32 | bytes 256 | tf_op jit(solution)/shard_map/psum | solution.py:32
  514.3 33.1 %psum.91 = f32[32]{0:T(128)S(1)} all-reduce(f32[32]{0:T(128)S(1)} %psum.90), channel_id=1, replica_groups=mesh['row'=16,'col'=16] {'row'}, use_global_device_ids=true, to_apply=%region_23.26 | all-reduce | flops 32 | bytes 256 | tf_op jit(solution)/shard_map/psum | solution.py:32
  548.4 30.9 %psum.92 = f32[32]{0:T(128)S(1)} all-reduce(f32[32]{0:T(128)S(1)} %get-tuple-element.10), channel_id=1, replica_groups=mesh['row'=16,'col'=16] {'col'}, use_global_device_ids=true, to_apply=%region_25.28 | all-reduce | flops 32 | bytes 256 | tf_op jit(solution)/shard_map/psum | solution.py:32
  579.2 28.5 %psum.93 = f32[32]{0:T(128)S(1)} all-reduce(f32[32]{0:T(128)S(1)} %psum.92), channel_id=1, replica_groups=mesh['row'=16,'col'=16] {'row'}, use_global_device_ids=true, to_apply=%region_26.29 | all-reduce | flops 32 | bytes 256 | tf_op jit(solution)/shard_map/psum | solution.py:32
  607.8 24.0 %all_gather.23 = f32[32,32,128]{2,1,0:T(8,128)S(1)} all-gather(f32[2,32,128]{2,1,0:T(8,128)S(1)} %multiply_add_fusion.2), channel_id=1, replica_groups=mesh['row'=16,'col'=16] {'col'}, dimensions={0}, use_global_device_ids=true | all-gather | bytes 557056 | tf_op jit(solution)/shard_map/all_gather | solution.py:60
  637.7 4.7 scatter_fusion.5
  643.2 19.1 %all_gather.22 = f32[32,32,128]{2,1,0:T(8,128)S(1)} all-gather(f32[2,32,128]{2,1,0:T(8,128)S(1)} %multiply_add_fusion.2), channel_id=1, replica_groups=mesh['row'=16,'col'=16] {'row'}, dimensions={0}, use_global_device_ids=true | all-gather | bytes 557056 | tf_op jit(solution)/shard_map/all_gather | solution.py:61
  663.7 5.3 fusion.1
  672.6 43.4 %reduce-scatter.19.cloned.1.call-done = f32[2,32,128]{2,1,0:T(8,128)} async-done(((f32[32,32,128]{2,1,0:T(8,128)}), f32[2,32,128]{2,1,0:T(8,128)}) %reduce-scatter.19.cloned.1.call-update) | async-done | bytes 32784 | tf_op jit(solution)/shard_map/reduce_scatter | solution.py:20
  716.0 57.2 %reduce-scatter.17.cloned.1.call-done = f32[2,32,128]{2,1,0:T(8,128)} async-done(((f32[32,32,128]{2,1,0:T(8,128)}), f32[2,32,128]{2,1,0:T(8,128)}) %reduce-scatter.17.cloned.1.call-update) | async-done | bytes 32784 | tf_op jit(solution)/shard_map/reduce_scatter | solution.py:20
  774.2 26.4 %psum.94 = f32[32]{0:T(128)S(1)} all-reduce(f32[32]{0:T(128)S(1)} %multiply_reduce_fusion), channel_id=1, replica_groups=mesh['row'=16,'col'=16] {'col'}, use_global_device_ids=true, to_apply=%region_32.35 | all-reduce | flops 32 | bytes 256 | tf_op jit(solution)/shard_map/psum | solution.py:32
  800.6 33.1 %psum.95 = f32[32]{0:T(128)S(1)} all-reduce(f32[32]{0:T(128)S(1)} %psum.94), channel_id=1, replica_groups=mesh['row'=16,'col'=16] {'row'}, use_global_device_ids=true, to_apply=%region_33.36 | all-reduce | flops 32 | bytes 256 | tf_op jit(solution)/shard_map/psum | solution.py:32
  (79 shorter events, 38.9 us)
Async XLA Ops:
  7.2 201.3 %reduce-scatter.11.cloned.1.call-start = ((), (), s32[]{:S(2)}) async-start(), calls=%async_computation.7 | async-start | bytes 557056 | tf_op jit(solution)/shard_map/reduce_scatter | solution.py:20
  33.0 10.9 %copy-start.7 = (f32[2,32,128]{2,1,0:T(8,128)S(1)}, f32[2,32,128]{2,1,0:T(8,128)}, u32[]{:S(2)}) copy-start(f32[2,32,128]{2,1,0:T(8,128)} %param.13) | copy-start | bytes 98308
  38.0 26.9 %copy-start = (f32[1,1,40,128,128]{4,3,2,1,0:T(8,128)S(1)}, f32[1,1,40,128,128]{4,3,2,1,0:T(8,128)}, u32[]{:S(2)}) copy-start(f32[1,1,40,128,128]{4,3,2,1,0:T(8,128)} %param.9) | copy-start | bytes 7864324
  42.9 0.8 copy-start.3
  43.8 164.7 %reduce-scatter.9.cloned.1.call-start = ((), (), s32[]{:S(2)}) async-start(), calls=%async_computation.6 | async-start | bytes 557056 | tf_op jit(solution)/shard_map/reduce_scatter | solution.py:20
  71.1 6.8 copy-start.10
  71.1 7.4 copy-start.9
  75.8 0.8 copy-start.4
  76.7 353.0 %reduce-scatter.15.cloned.1.call-start = ((), (), s32[]{:S(2)}) async-start(), calls=%async_computation.9 | async-start | bytes 557056 | tf_op jit(solution)/shard_map/reduce_scatter | solution.py:20
  80.4 128.1 %copy-start.8 = (f32[32]{0:T(128)S(1)}, f32[32]{0:T(128)}, u32[]{:S(2)}) copy-start(f32[32]{0:T(128)} %param.12) | copy-start | bytes 388
  360.1 0.8 copy-start.5
  361.0 125.9 %reduce-scatter.13.cloned.1.call-start = ((), (), s32[]{:S(2)}) async-start(), calls=%async_computation.8 | async-start | bytes 557056 | tf_op jit(solution)/shard_map/reduce_scatter | solution.py:20
  390.1 0.8 copy-start.6
  390.9 325.0 %reduce-scatter.19.cloned.1.call-start = ((), (), s32[]{:S(2)}) async-start(), calls=%async_computation.11 | async-start | bytes 557056 | tf_op jit(solution)/shard_map/reduce_scatter | solution.py:20
  642.4 0.8 copy-start.2
  643.2 130.0 %reduce-scatter.17.cloned.1.call-start = ((), (), s32[]{:S(2)}) async-start(), calls=%async_computation.10 | async-start | bytes 557056 | tf_op jit(solution)/shard_map/reduce_scatter | solution.py:20
  671.8 0.8 copy-start.1
Sparse Core Ops, SparseCore 0:
  43.9 73.4 reduce-scatter.10
  120.0 55.2 reduce-scatter.8
  361.1 68.5 reduce-scatter.14
  432.2 54.6 reduce-scatter.12
  643.3 72.6 reduce-scatter.18
  718.5 54.6 reduce-scatter.16
